TPU v7x, 256 devices: a whole 4x4x8 slice. The times are simulated.
256 devices in a mesh: pipe: 8 (over z), seq: 16 (over x, y), tp: 2 (over core).
Axes of the slice: x: 4, y: 4, z: 8, core: 2. Of those that a mesh axis runs over, the one named last changes fastest.
Arguments:
- layer_inputs: bfloat16 [8, 2048, 4096], P('pipe', ('seq', 'tp')), may hold values from -6 to 6
- out_grad: bfloat16 [2048, 4096], P('seq', 'tp'), may hold values from -6 to 6
- short_weights: bfloat16 [8, 7, 3, 4096], P('pipe', None, None, 'tp'), may hold values from -2 to 2
- long_filters: bfloat16 [8, 256, 128], P('pipe', 'tp'), may hold values from -0.15625 to 0.15625
- out_weights: bfloat16 [8, 4096, 4096], P('pipe', 'tp', 'seq'), may hold values from -0.09375 to 0.09375
Outputs:
- input_grad: bfloat16 [8, 2048, 4096], P('pipe', 'seq', 'tp')
- short_grad: float32 [8, 7, 3, 4096], P('pipe', None, None, 'tp')
- long_grad: float32 [8, 256, 128], P('pipe', 'tp')
All inputs are finite; a program needn't handle non-finite values.
Results may differ from a plain program's by a relative error of at most 0.03.
Values may be sent and summed in bfloat16 or wider, within the bound.
No kernel may reach another device: no remote copies, remote signals or barrier semaphores. Data moves between devices by JAX's collectives and lax.ppermute only.
A program may use at most 192 MiB of HBM per device.

v0:
```python
import jax
import jax.numpy as jnp
from jax import lax
from jax.sharding import PartitionSpec as P


def passed_along(array, axis, by):
    size = lax.axis_size(axis)
    pairs = [(i, i + by) for i in range(size) if 0 <= i + by < size]
    return lax.ppermute(array, axis, pairs)


def toeplitz_blocks(filters):
    groups, kernel_width = filters.shape
    base_row = jnp.concatenate(
        [
            jnp.zeros((groups, 1), filters.dtype),
            filters[:, ::-1],
            jnp.zeros((groups, kernel_width), filters.dtype),
        ],
        axis=1,
    )
    tiled = jnp.tile(base_row, (1, kernel_width))[:, : 2 * kernel_width * kernel_width]
    return tiled.reshape(groups, kernel_width, 2 * kernel_width)


def lag_sums(products):
    groups, kernel_width, window = products.shape
    flattened = products.reshape(groups, kernel_width * window)
    flattened = jnp.pad(flattened, ((0, 0), (0, kernel_width)))
    skewed = flattened.reshape(groups, kernel_width, window + 1)
    totals = jnp.sum(skewed, axis=1)
    return totals[:, 1 : kernel_width + 1][:, ::-1]


def to_groups(rows, groups):
    count = rows.shape[0]
    return jnp.transpose(rows.reshape(count, groups, rows.shape[1] // groups), (1, 2, 0))


def from_groups(blocks):
    groups, width, count = blocks.shape
    return jnp.transpose(blocks, (2, 0, 1)).reshape(count, groups * width)


def featurize(source, weights):
    tap_count = weights.shape[0]
    row_count = source.shape[0] - tap_count + 1
    running = jnp.zeros((weights.shape[1], row_count, source.shape[1]), jnp.float32)
    for offset in range(tap_count):
        start = tap_count - 1 - offset
        running = running + weights[offset][:, None, :] * source[start : start + row_count][None]
    return running


def spread_back(feature_grads, weights):
    tap_count = weights.shape[0]
    row_count = feature_grads.shape[1] - tap_count + 1
    running = jnp.zeros((row_count, feature_grads.shape[2]), jnp.float32)
    for offset in range(tap_count):
        running = running + jnp.sum(
            weights[offset][:, None, :] * feature_grads[:, offset : offset + row_count], axis=0
        )
    return running


def weight_grads(feature_grads, source):
    row_count = feature_grads.shape[1]
    tap_count = source.shape[0] - row_count + 1
    terms = []
    for offset in range(tap_count):
        start = tap_count - 1 - offset
        terms.append(jnp.sum(feature_grads * source[start : start + row_count][None], axis=1))
    return jnp.stack(terms)


def long_forward(padded, toeplitz, groups):
    grouped = to_groups(padded, groups)
    result = jnp.einsum("gis,gcs->gci", toeplitz, grouped, preferred_element_type=jnp.float32)
    return from_groups(result)


def long_backward(trailing, reversed_band, groups):
    grouped = to_groups(trailing, groups)
    result = jnp.einsum("grj,gcr->gcj", reversed_band, grouped, preferred_element_type=jnp.float32)
    return from_groups(result)


def filter_grads(mixed_grad, padded, groups):
    grad_groups = to_groups(mixed_grad, groups)
    value_groups = to_groups(padded, groups)
    products = jnp.einsum(
        "gci,gcs->gis", grad_groups, value_groups, preferred_element_type=jnp.float32
    )
    return lag_sums(products)


def recompute(layer_block, weights, filters):
    local_rows = lax.all_to_all(layer_block, "tp", split_axis=1, concat_axis=0, tiled=True)
    tap_count = weights.shape[0]
    kernel_width = filters.shape[1]
    before = passed_along(local_rows[local_rows.shape[0] - tap_count + 1 :], "seq", 1)
    extended = jnp.concatenate([before, local_rows], axis=0).astype(jnp.float32)
    features = featurize(extended, weights)
    products = (features[1] * features[2]).astype(jnp.bfloat16)
    earlier_products = passed_along(products[products.shape[0] - kernel_width + 1 :], "seq", 1)
    padded = jnp.concatenate(
        [jnp.zeros((1, products.shape[1]), jnp.bfloat16), earlier_products, products], axis=0
    )
    toeplitz = toeplitz_blocks(filters)
    reversed_band = jnp.concatenate(
        [toeplitz[:, :, kernel_width:], toeplitz[:, :, :kernel_width]], axis=1
    )
    mixed_rows = long_forward(padded, toeplitz, filters.shape[0])
    return (features, padded, reversed_band, mixed_rows, extended)


def dense_grad(incoming, columns, active):
    empty_sum = jnp.zeros((incoming.shape[0], columns.shape[0]), jnp.float32)
    piece = lax.all_gather(incoming, "tp", axis=1, tiled=True)
    summed = lax.cond(
        active,
        lambda: jnp.einsum("td,cd->tc", piece, columns, preferred_element_type=jnp.float32),
        lambda: empty_sum,
    )
    return summed.astype(jnp.bfloat16)


def backward(saved_state, incoming, dense_part, weights, groups, active):
    features, padded, reversed_band, mixed_rows, source = saved_state
    tap_count = weights.shape[0]
    kernel_width = reversed_band.shape[2]
    token_count, channels = incoming.shape
    edge_rows = tap_count - 1
    dense_float = dense_part.astype(jnp.float32)
    mixed_grad = (dense_float * features[0]).astype(jnp.bfloat16)
    after_grad = passed_along(mixed_grad[: kernel_width - 1], "seq", -1)
    trailing_grad = jnp.concatenate(
        [mixed_grad, after_grad, jnp.zeros((1, channels), jnp.bfloat16)], axis=0
    )

    def middle(operand):
        product_grad = long_backward(operand, reversed_band, groups)
        query_grad = dense_float * mixed_rows
        return (
            jnp.stack([query_grad, product_grad * features[2], product_grad * features[1]]),
            product_grad,
        )

    def middle_skipped(operand):
        return (
            jnp.zeros((3, token_count, channels), jnp.float32),
            jnp.zeros((token_count, channels), jnp.float32),
        )

    feature_grads, product_grad = lax.cond(active, middle, middle_skipped, trailing_grad)
    head_zeros = jnp.zeros((3, edge_rows, channels), jnp.float32)
    partial_sums = spread_back(
        jnp.concatenate([head_zeros, feature_grads[:, :edge_rows]], axis=1), weights
    )
    overflow = passed_along(partial_sums.astype(jnp.bfloat16), "seq", -1).astype(partial_sums.dtype)

    def finish(operands):
        grads, spill = operands
        trailing = jnp.concatenate([grads, head_zeros], axis=1)
        tail_rows = jnp.concatenate(
            [jnp.zeros((token_count - edge_rows, channels), jnp.float32), spill], axis=0
        )
        total = incoming.astype(jnp.float32) + spread_back(trailing, weights) + tail_rows
        return total.astype(jnp.bfloat16)

    def finish_skipped(operands):
        return jnp.zeros((token_count, channels), jnp.bfloat16)

    return (lax.cond(active, finish, finish_skipped, (feature_grads, overflow)), product_grad)


def per_device(layer_inputs, out_grad, short_weights, long_filters, out_weights):
    sections = lax.axis_size("pipe")
    section_index = lax.axis_index("pipe")
    weights = short_weights[0].astype(jnp.float32)
    filters = long_filters[0]
    groups = filters.shape[0]
    saved_state = recompute(layer_inputs[0], weights, filters)
    features, padded, reversed_band, mixed_rows, source = saved_state
    columns = lax.all_gather(out_weights[0], "seq", axis=1, tiled=True)
    incoming = out_grad
    input_result = jnp.zeros_like(out_grad)
    dense_kept = jnp.zeros(out_grad.shape, jnp.bfloat16)
    product_kept = jnp.zeros(out_grad.shape, jnp.float32)
    for step_index in range(sections):
        active = section_index == sections - 1 - step_index
        dense_part = dense_grad(incoming, columns, active)
        input_grad, product_grad = backward(
            saved_state, incoming, dense_part, weights, groups, active
        )
        input_result = jnp.where(active, input_grad, input_result)
        dense_kept = jnp.where(active, dense_part, dense_kept)
        product_kept = jnp.where(active, product_grad, product_kept)
        if step_index + 1 < sections:
            incoming = passed_along(input_grad, "pipe", -1)
    dense_float = dense_kept.astype(jnp.float32)
    mixed_grad = (dense_float * features[0]).astype(jnp.bfloat16)
    feature_grads = jnp.stack(
        [dense_float * mixed_rows, product_kept * features[2], product_kept * features[1]]
    )
    short_local = weight_grads(feature_grads, source)
    long_local = filter_grads(mixed_grad, padded, groups)
    short_result, long_result = (
        lax.psum(short_local.astype(jnp.bfloat16), "seq").astype(jnp.float32),
        lax.psum(long_local.astype(jnp.bfloat16), "seq").astype(jnp.float32),
    )
    return (input_result[None], short_result[None], long_result[None])


def solution(mesh):
    in_specs = (
        P("pipe", ("seq", "tp"), None),
        P("seq", "tp"),
        P("pipe", None, None, "tp"),
        P("pipe", "tp", None),
        P("pipe", "tp", "seq"),
    )
    out_specs = (P("pipe", "seq", "tp"), P("pipe", None, None, "tp"), P("pipe", "tp", None))
    return jax.shard_map(
        per_device, mesh=mesh, in_specs=in_specs, out_specs=out_specs, check_vma=False
    )
```

profile of v0, /device:TPU:32, one launch (start us, length us, event | category | flops | bytes accessed | tf_op | source)
XLA Modules:
  0.0 1389.2 jit_solution(17497464794075836733)
XLA Ops:
  22.8 13.0 tile.10
  42.9 12.5 copy.273
  88.4 68.1 %all-gather.27.cloned.1.call-done = bf16[1,2048,4096]{2,1,0:T(8,128)(2,1)} async-done(((bf16[1,2048,256]{2,1,0:T(8,128)(2,1)}), bf16[1,2048,4096]{2,1,0:T(8,128)(2,1)}) %all-gather.27.cloned.1.call-update) | async-done | bytes 16777232 | tf_op jit(solution)/shard_map/all_gather | solution.py:186
  197.7 9.4 multiply_reduce_fusion.110
  208.8 12.2 collective-permute-done.3
  225.3 10.5 collective-permute-done.4
  235.9 56.1 %all-gather.13.cloned.1.call-done = bf16[128,4096]{1,0:T(8,128)(2,1)} async-done(((bf16[128,2048]{1,0:T(8,128)(2,1)}), bf16[128,4096]{1,0:T(8,128)(2,1)}) %all-gather.13.cloned.1.call-update) | async-done | bytes 1048592 | tf_op jit(solution)/shard_map/all_gather | solution.py:120
  298.1 14.7 %collective-permute-done.5 = bf16[127,2048]{0,1:T(8,128)(2,1)S(1)} collective-permute-done((bf16[127,2048]{0,1:T(8,128)(2,1)S(1)}, bf16[127,2048]{0,1:T(8,128)(2,1)S(1)}, u32[]{:S(2)}, u32[]{:S(2)}) %collective-permute-start.5) | collective-permute-done | bytes 520224 | tf_op jit(solution)/shard_map/ppermute | solution.py:10
  319.0 9.7 multiply_reduce_fusion.104
  330.3 13.9 %collective-permute-done.6 = bf16[6,2048]{0,1:T(8,128)(2,1)S(1)} collective-permute-done((bf16[6,2048]{0,1:T(8,128)(2,1)S(1)}, bf16[6,2048]{0,1:T(8,128)(2,1)S(1)}, u32[]{:S(2)}, u32[]{:S(2)}) %collective-permute-start.6) | collective-permute-done | bytes 24608 | tf_op jit(solution)/shard_map/ppermute | solution.py:10
  349.0 12.0 collective-permute-done.7
  361.0 63.3 %all-gather.15.cloned.1.call-done = bf16[128,4096]{1,0:T(8,128)(2,1)} async-done(((bf16[128,2048]{1,0:T(8,128)(2,1)}), bf16[128,4096]{1,0:T(8,128)(2,1)}) %all-gather.15.cloned.1.call-update) | async-done | bytes 1048592 | tf_op jit(solution)/shard_map/all_gather | solution.py:120
  430.1 14.7 %collective-permute-done.8 = bf16[127,2048]{0,1:T(8,128)(2,1)S(1)} collective-permute-done((bf16[127,2048]{0,1:T(8,128)(2,1)S(1)}, bf16[127,2048]{0,1:T(8,128)(2,1)S(1)}, u32[]{:S(2)}, u32[]{:S(2)}) %collective-permute-start.8) | collective-permute-done | bytes 520224 | tf_op jit(solution)/shard_map/ppermute | solution.py:10
  451.2 9.7 multiply_reduce_fusion.98
  462.6 13.9 %collective-permute-done.9 = bf16[6,2048]{0,1:T(8,128)(2,1)S(1)} collective-permute-done((bf16[6,2048]{0,1:T(8,128)(2,1)S(1)}, bf16[6,2048]{0,1:T(8,128)(2,1)S(1)}, u32[]{:S(2)}, u32[]{:S(2)}) %collective-permute-start.9) | collective-permute-done | bytes 24608 | tf_op jit(solution)/shard_map/ppermute | solution.py:10
  481.0 12.0 collective-permute-done.10
  493.1 64.1 %all-gather.17.cloned.1.call-done = bf16[128,4096]{1,0:T(8,128)(2,1)} async-done(((bf16[128,2048]{1,0:T(8,128)(2,1)}), bf16[128,4096]{1,0:T(8,128)(2,1)}) %all-gather.17.cloned.1.call-update) | async-done | bytes 1048592 | tf_op jit(solution)/shard_map/all_gather | solution.py:120
  562.9 14.7 %collective-permute-done.11 = bf16[127,2048]{0,1:T(8,128)(2,1)S(1)} collective-permute-done((bf16[127,2048]{0,1:T(8,128)(2,1)S(1)}, bf16[127,2048]{0,1:T(8,128)(2,1)S(1)}, u32[]{:S(2)}, u32[]{:S(2)}) %collective-permute-start.11) | collective-permute-done | bytes 520224 | tf_op jit(solution)/shard_map/ppermute | solution.py:10
  584.3 9.7 multiply_reduce_fusion.92
  595.6 13.9 %collective-permute-done.12 = bf16[6,2048]{0,1:T(8,128)(2,1)S(1)} collective-permute-done((bf16[6,2048]{0,1:T(8,128)(2,1)S(1)}, bf16[6,2048]{0,1:T(8,128)(2,1)S(1)}, u32[]{:S(2)}, u32[]{:S(2)}) %collective-permute-start.12) | collective-permute-done | bytes 24608 | tf_op jit(solution)/shard_map/ppermute | solution.py:10
  614.1 12.0 collective-permute-done.13
  626.1 65.0 %all-gather.19.cloned.1.call-done = bf16[128,4096]{1,0:T(8,128)(2,1)} async-done(((bf16[128,2048]{1,0:T(8,128)(2,1)}), bf16[128,4096]{1,0:T(8,128)(2,1)}) %all-gather.19.cloned.1.call-update) | async-done | bytes 1048592 | tf_op jit(solution)/shard_map/all_gather | solution.py:120
  696.9 14.7 %collective-permute-done.14 = bf16[127,2048]{0,1:T(8,128)(2,1)S(1)} collective-permute-done((bf16[127,2048]{0,1:T(8,128)(2,1)S(1)}, bf16[127,2048]{0,1:T(8,128)(2,1)S(1)}, u32[]{:S(2)}, u32[]{:S(2)}) %collective-permute-start.14) | collective-permute-done | bytes 520224 | tf_op jit(solution)/shard_map/ppermute | solution.py:10
  717.9 9.7 multiply_reduce_fusion.86
  729.2 13.9 %collective-permute-done.15 = bf16[6,2048]{0,1:T(8,128)(2,1)S(1)} collective-permute-done((bf16[6,2048]{0,1:T(8,128)(2,1)S(1)}, bf16[6,2048]{0,1:T(8,128)(2,1)S(1)}, u32[]{:S(2)}, u32[]{:S(2)}) %collective-permute-start.15) | collective-permute-done | bytes 24608 | tf_op jit(solution)/shard_map/ppermute | solution.py:10
  747.9 12.0 collective-permute-done.16
  759.9 64.0 %all-gather.21.cloned.1.call-done = bf16[128,4096]{1,0:T(8,128)(2,1)} async-done(((bf16[128,2048]{1,0:T(8,128)(2,1)}), bf16[128,4096]{1,0:T(8,128)(2,1)}) %all-gather.21.cloned.1.call-update) | async-done | bytes 1048592 | tf_op jit(solution)/shard_map/all_gather | solution.py:120
  829.6 14.7 %collective-permute-done.17 = bf16[127,2048]{0,1:T(8,128)(2,1)S(1)} collective-permute-done((bf16[127,2048]{0,1:T(8,128)(2,1)S(1)}, bf16[127,2048]{0,1:T(8,128)(2,1)S(1)}, u32[]{:S(2)}, u32[]{:S(2)}) %collective-permute-start.17) | collective-permute-done | bytes 520224 | tf_op jit(solution)/shard_map/ppermute | solution.py:10
  850.9 9.7 multiply_reduce_fusion.80
  862.3 13.9 %collective-permute-done.18 = bf16[6,2048]{0,1:T(8,128)(2,1)S(1)} collective-permute-done((bf16[6,2048]{0,1:T(8,128)(2,1)S(1)}, bf16[6,2048]{0,1:T(8,128)(2,1)S(1)}, u32[]{:S(2)}, u32[]{:S(2)}) %collective-permute-start.18) | collective-permute-done | bytes 24608 | tf_op jit(solution)/shard_map/ppermute | solution.py:10
  880.8 57.0 %collective-permute-done.19 = bf16[128,2048]{1,0:T(8,128)(2,1)} collective-permute-done((bf16[128,2048]{1,0:T(8,128)(2,1)}, bf16[128,2048]{1,0:T(8,128)(2,1)}, u32[]{:S(2)}, u32[]{:S(2)}) %collective-permute-start.19) | collective-permute-done | bytes 524320 | tf_op jit(solution)/shard_map/ppermute | solution.py:10
  937.8 16.7 %all-gather.23.cloned.1.call-done = bf16[128,4096]{1,0:T(8,128)(2,1)} async-done(((bf16[128,2048]{1,0:T(8,128)(2,1)}), bf16[128,4096]{1,0:T(8,128)(2,1)}) %all-gather.23.cloned.1.call-update) | async-done | bytes 1048592 | tf_op jit(solution)/shard_map/all_gather | solution.py:120
  954.5 17.2 %conditional.42 = (f32[128,2048]{1,0:T(8,128)}, f32[128,2048]{0,1:T(8,128)}, bf16[128,2048]{0,1:T(8,128)(2,1)}) conditional(s32[]{:T(128)} %convert_element_type.283, () %tuple.255, (bf16[128,4096]{1,0:T(8,128)(2,1)}, bf16[2048,4096]{1,0:T(8,128)(2,1)}) %tuple.637), branch_computations={%region_115.116_spmd, %region_116.117_spmd} | conditional | flops 2148007936 | bytes 22020120 | solution.py:121
  954.5 12.9 fusion.9
  974.4 14.7 %collective-permute-done.20 = bf16[127,2048]{0,1:T(8,128)(2,1)S(1)} collective-permute-done((bf16[127,2048]{0,1:T(8,128)(2,1)S(1)}, bf16[127,2048]{0,1:T(8,128)(2,1)S(1)}, u32[]{:S(2)}, u32[]{:S(2)}) %collective-permute-start.20) | collective-permute-done | bytes 520224 | tf_op jit(solution)/shard_map/ppermute | solution.py:10
  990.5 13.2 conditional.43
  1006.6 9.7 multiply_reduce_fusion.74
  1017.9 13.9 %collective-permute-done.21 = bf16[6,2048]{0,1:T(8,128)(2,1)S(1)} collective-permute-done((bf16[6,2048]{0,1:T(8,128)(2,1)S(1)}, bf16[6,2048]{0,1:T(8,128)(2,1)S(1)}, u32[]{:S(2)}, u32[]{:S(2)}) %collective-permute-start.21) | collective-permute-done | bytes 24608 | tf_op jit(solution)/shard_map/ppermute | solution.py:10
  1032.9 20.9 %conditional.44 = (bf16[128,2048]{1,0:T(8,128)(2,1)}) conditional(s32[]{:T(128)} %convert_element_type.283, () %tuple.217, (bf16[128,2048]{1,0:T(8,128)(2,1)}, f32[7,3,2048]{2,1,0:T(4,128)S(1)}, f32[3,128,2048]{1,2,0:T(8,128)}, f32[6,2048]{0,1:T(8,128)}) %tuple.258), branch_computations={%region_125.126_spmd, %region_126.134_spmd} | conditional | flops 11796480 | bytes 26026020 | solution.py:175
  1039.3 11.9 multiply_reduce_fusion.47
  1055.7 12.7 collective-permute-done.22
  1099.4 17.8 %copy.274 = f32[128,128,256]{0,2,1:T(8,128)} copy(f32[128,128,256]{2,1,0:T(8,128)} %fusion.30) | data formatting | bytes 33554432 | tf_op jit(solution)/shard_map/reshape | solution.py:29
  1117.2 13.3 pad.28
  1130.5 17.5 %reshape.203 = f32[128,128,257]{0,2,1:T(8,128)} reshape(f32[128,32896]{0,1:T(8,128)} %pad.28) | data formatting | bytes 33685504 | tf_op jit(solution)/shard_map/reshape | solution.py:31
  1158.1 77.1 %psum.15 = bf16[1,128,128]{1,2,0:T(8,128)(2,1)} all-reduce(bf16[1,128,128]{1,2,0:T(8,128)(2,1)} %bitcast.399), channel_id=1, replica_groups=mesh['pipe'=8,'seq'=16,'tp'=2] {'seq'}, use_global_device_ids=true, to_apply=%region_162.163 | all-reduce | flops 16384 | bytes 65536 | tf_op jit(solution)/shard_map/psum | solution.py:211
  1256.4 9.4 multiply_reduce_fusion.68
  1268.4 8.9 collective-permute-done.24
  1280.5 99.8 %all-reduce.27.cloned.1.call-done = bf16[1,7,3,2048]{3,1,2,0:T(8,128)(2,1)} async-done(((bf16[1,7,3,2048]{3,1,2,0:T(8,128)(2,1)}), bf16[1,7,3,2048]{3,1,2,0:T(8,128)(2,1)}) %all-reduce.27.cloned.1.call-update) | async-done | bytes 86032 | tf_op jit(solution)/shard_map/psum | solution.py:210
  (283 shorter events, 344.9 us)
Async XLA Ops:
  7.2 10.9 copy-start.64
  7.2 81.3 %all-gather.11.cloned.1.call-start = ((), (), s32[]{:S(2)}) async-start(), calls=%async_computation.1 | async-start | bytes 1572864 | tf_op jit(solution)/shard_map/all_gather | solution.py:120
  7.9 148.7 %all-gather.27.cloned.1.call-start = ((), (), s32[]{:S(2)}) async-start(), calls=%async_computation.10 | async-start | bytes 17825792 | tf_op jit(solution)/shard_map/all_gather | solution.py:186
  8.7 283.3 %all-gather.13.cloned.1.call-start = ((), (), s32[]{:S(2)}) async-start(), calls=%async_computation.2 | async-start | bytes 1572864 | tf_op jit(solution)/shard_map/all_gather | solution.py:120
  14.5 47.9 %collective-permute-start = (bf16[6,2048]{1,0:T(8,128)(2,1)S(1)}, bf16[6,2048]{1,0:T(8,128)(2,1)S(1)}, u32[]{:S(2)}, u32[]{:S(2)}) collective-permute-start(bf16[6,2048]{1,0:T(8,128)(2,1)S(1)} %slice.757), channel_id=1, source_target_pairs={{0,2},{2,4},{4,6},{6,8},{8,10},{10,12},{12,14},{14,16},{16,18},{18... | collective-permute-start | bytes 73736 | tf_op jit(solution)/shard_map/ppermute | solution.py:10
  42.9 12.5 copy-start.63
  70.5 7.7 copy-start.32
  163.8 13.7 collective-permute-start.1
  167.7 14.7 %collective-permute-start.2 = (bf16[127,2048]{0,1:T(8,128)(2,1)}, bf16[127,2048]{0,1:T(8,128)(2,1)}, u32[]{:S(2)}, u32[]{:S(2)}) collective-permute-start(bf16[127,2048]{0,1:T(8,128)(2,1)} %bitcast.344), channel_id=1, source_target_pairs={{2,0},{4,2},{6,4},{8,6},{10,8},{12,10},{14,12},{16,14},{18,16},{20... | collective-permute-start | bytes 1560584 | tf_op jit(solution)/shard_map/ppermute | solution.py:10
  183.2 9.6 slice-start
  185.7 7.1 copy-start.1
  185.8 7.1 slice-start.1
  207.5 13.5 collective-permute-start.3
  222.9 12.9 collective-permute-start.4
  235.8 188.6 %all-gather.15.cloned.1.call-start = ((), (), s32[]{:S(2)}) async-start(), calls=%async_computation.3 | async-start | bytes 1572864 | tf_op jit(solution)/shard_map/all_gather | solution.py:120
  296.8 16.0 %collective-permute-start.5 = (bf16[127,2048]{0,1:T(8,128)(2,1)S(1)}, bf16[127,2048]{0,1:T(8,128)(2,1)S(1)}, u32[]{:S(2)}, u32[]{:S(2)}) collective-permute-start(bf16[127,2048]{0,1:T(8,128)(2,1)S(1)} %bitcast.392), channel_id=1, source_target_pairs={{2,0},{4,2},{6,4},{8,6},{10,8},{12,10},{14,12},{16,14},{18,16},{20... | collective-permute-start | bytes 1560584 | tf_op jit(solution)/shard_map/ppermute | solution.py:10
  316.2 2.8 copy-start.8
  329.0 15.2 %collective-permute-start.6 = (bf16[6,2048]{0,1:T(8,128)(2,1)S(1)}, bf16[6,2048]{0,1:T(8,128)(2,1)S(1)}, u32[]{:S(2)}, u32[]{:S(2)}) collective-permute-start(bf16[6,2048]{0,1:T(8,128)(2,1)S(1)} %add_convert_fusion.14), channel_id=1, source_target_pairs={{2,0},{4,2},{6,4},{8,6},{10,8},{12,10},{14,12},{16,14},{18,16},{20... | collective-permute-start | bytes 73736 | tf_op jit(solution)/shard_map/ppermute | solution.py:10
  346.4 14.6 %collective-permute-start.7 = (bf16[128,2048]{1,0:T(8,128)(2,1)}, bf16[128,2048]{1,0:T(8,128)(2,1)}, u32[]{:S(2)}, u32[]{:S(2)}) collective-permute-start(bf16[128,2048]{1,0:T(8,128)(2,1)} %get-tuple-element.1088), channel_id=1, source_target_pairs={{32,0},{64,32},{96,64},{128,96},{160,128},{192,160},{224,192},{33,... | collective-permute-start | bytes 1572872 | tf_op jit(solution)/shard_map/ppermute | solution.py:10
  361.0 196.2 %all-gather.17.cloned.1.call-start = ((), (), s32[]{:S(2)}) async-start(), calls=%async_computation.4 | async-start | bytes 1572864 | tf_op jit(solution)/shard_map/all_gather | solution.py:120
  428.8 16.0 %collective-permute-start.8 = (bf16[127,2048]{0,1:T(8,128)(2,1)S(1)}, bf16[127,2048]{0,1:T(8,128)(2,1)S(1)}, u32[]{:S(2)}, u32[]{:S(2)}) collective-permute-start(bf16[127,2048]{0,1:T(8,128)(2,1)S(1)} %bitcast.393), channel_id=1, source_target_pairs={{2,0},{4,2},{6,4},{8,6},{10,8},{12,10},{14,12},{16,14},{18,16},{20... | collective-permute-start | bytes 1560584 | tf_op jit(solution)/shard_map/ppermute | solution.py:10
  448.4 2.8 copy-start.11
  461.3 15.2 %collective-permute-start.9 = (bf16[6,2048]{0,1:T(8,128)(2,1)S(1)}, bf16[6,2048]{0,1:T(8,128)(2,1)S(1)}, u32[]{:S(2)}, u32[]{:S(2)}) collective-permute-start(bf16[6,2048]{0,1:T(8,128)(2,1)S(1)} %add_convert_fusion.13), channel_id=1, source_target_pairs={{2,0},{4,2},{6,4},{8,6},{10,8},{12,10},{14,12},{16,14},{18,16},{20... | collective-permute-start | bytes 73736 | tf_op jit(solution)/shard_map/ppermute | solution.py:10
  478.4 14.6 %collective-permute-start.10 = (bf16[128,2048]{1,0:T(8,128)(2,1)}, bf16[128,2048]{1,0:T(8,128)(2,1)}, u32[]{:S(2)}, u32[]{:S(2)}) collective-permute-start(bf16[128,2048]{1,0:T(8,128)(2,1)} %get-tuple-element.1089), channel_id=1, source_target_pairs={{32,0},{64,32},{96,64},{128,96},{160,128},{192,160},{224,192},{33,... | collective-permute-start | bytes 1572872 | tf_op jit(solution)/shard_map/ppermute | solution.py:10
  493.0 198.1 %all-gather.19.cloned.1.call-start = ((), (), s32[]{:S(2)}) async-start(), calls=%async_computation.5 | async-start | bytes 1572864 | tf_op jit(solution)/shard_map/all_gather | solution.py:120
  561.6 16.0 %collective-permute-start.11 = (bf16[127,2048]{0,1:T(8,128)(2,1)S(1)}, bf16[127,2048]{0,1:T(8,128)(2,1)S(1)}, u32[]{:S(2)}, u32[]{:S(2)}) collective-permute-start(bf16[127,2048]{0,1:T(8,128)(2,1)S(1)} %bitcast.394), channel_id=1, source_target_pairs={{2,0},{4,2},{6,4},{8,6},{10,8},{12,10},{14,12},{16,14},{18,16},{20... | collective-permute-start | bytes 1560584 | tf_op jit(solution)/shard_map/ppermute | solution.py:10
  594.3 15.2 %collective-permute-start.12 = (bf16[6,2048]{0,1:T(8,128)(2,1)S(1)}, bf16[6,2048]{0,1:T(8,128)(2,1)S(1)}, u32[]{:S(2)}, u32[]{:S(2)}) collective-permute-start(bf16[6,2048]{0,1:T(8,128)(2,1)S(1)} %add_convert_fusion.12), channel_id=1, source_target_pairs={{2,0},{4,2},{6,4},{8,6},{10,8},{12,10},{14,12},{16,14},{18,16},{20... | collective-permute-start | bytes 73736 | tf_op jit(solution)/shard_map/ppermute | solution.py:10
  611.4 14.6 %collective-permute-start.13 = (bf16[128,2048]{1,0:T(8,128)(2,1)}, bf16[128,2048]{1,0:T(8,128)(2,1)}, u32[]{:S(2)}, u32[]{:S(2)}) collective-permute-start(bf16[128,2048]{1,0:T(8,128)(2,1)} %get-tuple-element.1090), channel_id=1, source_target_pairs={{32,0},{64,32},{96,64},{128,96},{160,128},{192,160},{224,192},{33,... | collective-permute-start | bytes 1572872 | tf_op jit(solution)/shard_map/ppermute | solution.py:10
  626.1 197.9 %all-gather.21.cloned.1.call-start = ((), (), s32[]{:S(2)}) async-start(), calls=%async_computation.6 | async-start | bytes 1572864 | tf_op jit(solution)/shard_map/all_gather | solution.py:120
  695.6 16.0 %collective-permute-start.14 = (bf16[127,2048]{0,1:T(8,128)(2,1)S(1)}, bf16[127,2048]{0,1:T(8,128)(2,1)S(1)}, u32[]{:S(2)}, u32[]{:S(2)}) collective-permute-start(bf16[127,2048]{0,1:T(8,128)(2,1)S(1)} %bitcast.395), channel_id=1, source_target_pairs={{2,0},{4,2},{6,4},{8,6},{10,8},{12,10},{14,12},{16,14},{18,16},{20... | collective-permute-start | bytes 1560584 | tf_op jit(solution)/shard_map/ppermute | solution.py:10
  715.0 2.8 copy-start.17
  727.9 15.2 %collective-permute-start.15 = (bf16[6,2048]{0,1:T(8,128)(2,1)S(1)}, bf16[6,2048]{0,1:T(8,128)(2,1)S(1)}, u32[]{:S(2)}, u32[]{:S(2)}) collective-permute-start(bf16[6,2048]{0,1:T(8,128)(2,1)S(1)} %add_convert_fusion.11), channel_id=1, source_target_pairs={{2,0},{4,2},{6,4},{8,6},{10,8},{12,10},{14,12},{16,14},{18,16},{20... | collective-permute-start | bytes 73736 | tf_op jit(solution)/shard_map/ppermute | solution.py:10
  745.2 14.6 %collective-permute-start.16 = (bf16[128,2048]{1,0:T(8,128)(2,1)}, bf16[128,2048]{1,0:T(8,128)(2,1)}, u32[]{:S(2)}, u32[]{:S(2)}) collective-permute-start(bf16[128,2048]{1,0:T(8,128)(2,1)} %get-tuple-element.1091), channel_id=1, source_target_pairs={{32,0},{64,32},{96,64},{128,96},{160,128},{192,160},{224,192},{33,... | collective-permute-start | bytes 1572872 | tf_op jit(solution)/shard_map/ppermute | solution.py:10
  759.9 194.7 %all-gather.23.cloned.1.call-start = ((), (), s32[]{:S(2)}) async-start(), calls=%async_computation.7 | async-start | bytes 1572864 | tf_op jit(solution)/shard_map/all_gather | solution.py:120
  828.3 16.0 %collective-permute-start.17 = (bf16[127,2048]{0,1:T(8,128)(2,1)S(1)}, bf16[127,2048]{0,1:T(8,128)(2,1)S(1)}, u32[]{:S(2)}, u32[]{:S(2)}) collective-permute-start(bf16[127,2048]{0,1:T(8,128)(2,1)S(1)} %bitcast.396), channel_id=1, source_target_pairs={{2,0},{4,2},{6,4},{8,6},{10,8},{12,10},{14,12},{16,14},{18,16},{20... | collective-permute-start | bytes 1560584 | tf_op jit(solution)/shard_map/ppermute | solution.py:10
  861.0 15.2 %collective-permute-start.18 = (bf16[6,2048]{0,1:T(8,128)(2,1)S(1)}, bf16[6,2048]{0,1:T(8,128)(2,1)S(1)}, u32[]{:S(2)}, u32[]{:S(2)}) collective-permute-start(bf16[6,2048]{0,1:T(8,128)(2,1)S(1)} %add_convert_fusion.10), channel_id=1, source_target_pairs={{2,0},{4,2},{6,4},{8,6},{10,8},{12,10},{14,12},{16,14},{18,16},{20... | collective-permute-start | bytes 73736 | tf_op jit(solution)/shard_map/ppermute | solution.py:10
  878.1 59.6 %collective-permute-start.19 = (bf16[128,2048]{1,0:T(8,128)(2,1)}, bf16[128,2048]{1,0:T(8,128)(2,1)}, u32[]{:S(2)}, u32[]{:S(2)}) collective-permute-start(bf16[128,2048]{1,0:T(8,128)(2,1)} %get-tuple-element.1092), channel_id=1, source_target_pairs={{32,0},{64,32},{96,64},{128,96},{160,128},{192,160},{224,192},{33,... | collective-permute-start | bytes 1572872 | tf_op jit(solution)/shard_map/ppermute | solution.py:10
  937.8 146.2 %all-gather.25.cloned.1.call-start = ((), (), s32[]{:S(2)}) async-start(), calls=%async_computation.8 | async-start | bytes 1572864 | tf_op jit(solution)/shard_map/all_gather | solution.py:120
  973.1 16.0 %collective-permute-start.20 = (bf16[127,2048]{0,1:T(8,128)(2,1)S(1)}, bf16[127,2048]{0,1:T(8,128)(2,1)S(1)}, u32[]{:S(2)}, u32[]{:S(2)}) collective-permute-start(bf16[127,2048]{0,1:T(8,128)(2,1)S(1)} %bitcast.397), channel_id=1, source_target_pairs={{2,0},{4,2},{6,4},{8,6},{10,8},{12,10},{14,12},{16,14},{18,16},{20... | collective-permute-start | bytes 1560584 | tf_op jit(solution)/shard_map/ppermute | solution.py:10
  1003.7 2.8 copy-start.23
  1016.6 15.2 %collective-permute-start.21 = (bf16[6,2048]{0,1:T(8,128)(2,1)S(1)}, bf16[6,2048]{0,1:T(8,128)(2,1)S(1)}, u32[]{:S(2)}, u32[]{:S(2)}) collective-permute-start(bf16[6,2048]{0,1:T(8,128)(2,1)S(1)} %add_convert_fusion.9), channel_id=1, source_target_pairs={{2,0},{4,2},{6,4},{8,6},{10,8},{12,10},{14,12},{16,14},{18,16},{20... | collective-permute-start | bytes 73736 | tf_op jit(solution)/shard_map/ppermute | solution.py:10
  1039.3 11.9 copy-start.58
  1053.8 14.6 %collective-permute-start.22 = (bf16[128,2048]{1,0:T(8,128)(2,1)}, bf16[128,2048]{1,0:T(8,128)(2,1)}, u32[]{:S(2)}, u32[]{:S(2)}) collective-permute-start(bf16[128,2048]{1,0:T(8,128)(2,1)} %get-tuple-element.1093), channel_id=1, source_target_pairs={{32,0},{64,32},{96,64},{128,96},{160,128},{192,160},{224,192},{33,... | collective-permute-start | bytes 1572872 | tf_op jit(solution)/shard_map/ppermute | solution.py:10
  1068.4 311.9 %all-reduce.27.cloned.1.call-start = ((), (), s32[]{:S(2)}) async-start(), calls=%async_computation.9 | async-start | bytes 196608 | tf_op jit(solution)/shard_map/psum | solution.py:210
  1087.2 4.1 copy-start.2
  1090.0 149.2 %collective-permute-start.23 = (bf16[127,2048]{0,1:T(8,128)(2,1)}, bf16[127,2048]{0,1:T(8,128)(2,1)}, u32[]{:S(2)}, u32[]{:S(2)}) collective-permute-start(bf16[127,2048]{0,1:T(8,128)(2,1)} %bitcast.351), channel_id=1, source_target_pairs={{2,0},{4,2},{6,4},{8,6},{10,8},{12,10},{14,12},{16,14},{18,16},{20... | collective-permute-start | bytes 1560584 | tf_op jit(solution)/shard_map/ppermute | solution.py:10
  1248.0 5.9 copy-start.50
  1266.2 11.1 collective-permute-start.24
  (17 other events, 34.6 us)
Sparse Core Ops, SparseCore 0:
  9.8 16.9 all-gather.10
  29.2 127.3 all-gather.26
  235.9 55.9 all-gather.12
  361.1 63.2 all-gather.14
  493.1 63.9 all-gather.16
  626.2 64.8 all-gather.18
  760.0 63.8 all-gather.20
  937.9 16.6 all-gather.22
  1068.5 15.4 all-gather.24
  1268.5 111.7 all-reduce.26
where the time goes:
time: 1400 us; the launch traced here: 1390 us
  waiting for transfers between devices  826 us (59%)
  local copies, waits for them, and re-layouts  195 us (14%)
  other arithmetic  189 us (14%)
  blocking collectives  81.3 us (6%)
  starting transfers between devices  45.8 us (3%)
  matrix products  32.7 us (2%)
  between operations  15.6 us (1%)
    all_gather x8, waiting for transfers between devices, dense_grad(): piece = lax.all_gather(incoming, 'tp', axis=1, tiled=True)  330 us
    ppermute x25, waiting for transfers between devices, passed_along(): return lax.ppermute(array, axis, pairs)  327 us
    psum x1, waiting for transfers between devices, per_device(): lax.psum(short_local.astype(jnp.bfloat16), 'seq').astype(jnp.float32)  99.8 us
    reduce_sum x10, other arithmetic, spread_back(): jnp.sum(weights[offset][:, None, :] * feature_grads[:, offset:offset + ro...  88.6 us
    psum x1, blocking collectives, per_device(): lax.psum(long_local.astype(jnp.bfloat16), 'seq').astype(jnp.float32)  77.1 us
    all_gather x1, waiting for transfers between devices, per_device(): columns = lax.all_gather(out_weights[0], 'seq', axis=1, tiled=True)  68.1 us
    another operation x46, local copies, waits for them, and re-layouts  50.6 us
    ppermute x25, starting transfers between devices, passed_along(): return lax.ppermute(array, axis, pairs)  45.4 us
  transfers between devices with their start and end apart: 35, of which 32 were waited for; matrix products, arithmetic and copies ran while one was open for 12% of the time, Pallas kernels for 0%

commit v1 on v0

--- a/solution.py
+++ b/solution.py
@@ -183,7 +183,8 @@
     groups = filters.shape[0]
     saved_state = recompute(layer_inputs[0], weights, filters)
     features, padded, reversed_band, mixed_rows, source = saved_state
-    columns = lax.all_gather(out_weights[0], "seq", axis=1, tiled=True)
+    copies = jnp.concatenate([out_weights[0]] * lax.axis_size("seq"), axis=1)
+    columns = lax.all_to_all(copies, "seq", 1, 1, tiled=True)
     incoming = out_grad
     input_result = jnp.zeros_like(out_grad)
     dense_kept = jnp.zeros(out_grad.shape, jnp.bfloat16)

time: 1400 us -> 1560 us (1.11)
  waiting for transfers between devices: 826 us -> 954 us
  local copies, waits for them, and re-layouts: 195 us -> 223 us
    all_to_all x0 -> x1, waiting for transfers between devices: none -> 123 us  [per_device(): columns = lax.all_to_all(copies, 'seq', 1, 1, tiled=True)]
    ppermute x25, waiting for transfers between devices: 327 us -> 421 us  [passed_along(): return lax.ppermute(array, axis, pairs)]
    all_gather x1 -> x0, waiting for transfers between devices: 68.1 us -> none  [per_device(): columns = lax.all_gather(out_weights[0], 'seq', axis=1, tiled=True)]
    all_to_all x0 -> x1, local copies, waits for them, and re-layouts: none -> 21.6 us  [per_device(): columns = lax.all_to_all(copies, 'seq', 1, 1, tiled=True)]
    all_gather x8, waiting for transfers between devices: 330 us -> 313 us  [dense_grad(): piece = lax.all_gather(incoming, 'tp', axis=1, tiled=True)]
  transfers between devices with their start and end apart: 35 -> 35, of which waited for: 32 -> 33; matrix products, arithmetic and copies ran while one was open for 12% -> 12% of each run, Pallas kernels for 0% -> 0%
where the time goes in v1:
time: 1560 us; the launch traced here: 1550 us
  waiting for transfers between devices  954 us (61%)
  local copies, waits for them, and re-layouts  223 us (14%)
  other arithmetic  189 us (12%)
  blocking collectives  81.3 us (5%)
  starting transfers between devices  57.8 us (4%)
  matrix products  29.5 us (2%)
    ppermute x25, waiting for transfers between devices, passed_along(): return lax.ppermute(array, axis, pairs)  421 us
    all_gather x8, waiting for transfers between devices, dense_grad(): piece = lax.all_gather(incoming, 'tp', axis=1, tiled=True)  313 us
    all_to_all x1, waiting for transfers between devices, per_device(): columns = lax.all_to_all(copies, 'seq', 1, 1, tiled=True)  123 us
    psum x1, waiting for transfers between devices, per_device(): lax.psum(short_local.astype(jnp.bfloat16), 'seq').astype(jnp.float32)  96.5 us
    reduce_sum x10, other arithmetic, spread_back(): jnp.sum(weights[offset][:, None, :] * feature_grads[:, offset:offset + ro...  88.7 us
    psum x1, blocking collectives, per_device(): lax.psum(long_local.astype(jnp.bfloat16), 'seq').astype(jnp.float32)  77.1 us
    another operation x46, local copies, waits for them, and re-layouts  50.5 us
    ppermute x25, starting transfers between devices, passed_along(): return lax.ppermute(array, axis, pairs)  50 us
  transfers between devices with their start and end apart: 35, of which 33 were waited for; matrix products, arithmetic and copies ran while one was open for 12% of the time, Pallas kernels for 0%

profile of v1, /device:TPU:32, one launch (start us, length us, event | category | flops | bytes accessed | tf_op | source)
XLA Modules:
  0.0 1551.5 jit_solution(1414279517346782488)
XLA Ops:
  35.5 13.0 tile.10
  55.6 12.6 copy.354
  75.1 98.5 %collective-permute-done = bf16[6,2048]{1,0:T(8,128)(2,1)S(1)} collective-permute-done((bf16[6,2048]{1,0:T(8,128)(2,1)S(1)}, bf16[6,2048]{1,0:T(8,128)(2,1)S(1)}, u32[]{:S(2)}, u32[]{:S(2)}) %collective-permute-start) | collective-permute-done | bytes 24608 | tf_op jit(solution)/shard_map/ppermute | solution.py:10
  199.6 122.6 %all-to-all-done = bf16[2048,16,256]{2,0,1:T(8,128)(2,1)} async-done(((bf16[2048,16,256]{2,0,1:T(8,128)(2,1)}), bf16[2048,16,256]{2,0,1:T(8,128)(2,1)}, u32[]{:S(2)}, u32[]{:S(2)}) %all-to-all-start) | async-done | bytes 16777248 | tf_op jit(solution)/shard_map/all_to_all | solution.py:187
  322.1 21.6 %copy.274 = bf16[2048,16,256]{0,2,1:T(8,128)(2,1)} copy(bf16[2048,16,256]{2,0,1:T(8,128)(2,1)} %all-to-all-done) | data formatting | bytes 33554432 | tf_op jit(solution)/shard_map/all_to_all | solution.py:187
  399.1 12.2 collective-permute-done.3
  416.2 10.0 collective-permute-done.4
  426.4 53.1 %all-gather.11.cloned.1.call-done = bf16[128,4096]{1,0:T(8,128)(2,1)} async-done(((bf16[128,2048]{1,0:T(8,128)(2,1)}), bf16[128,4096]{1,0:T(8,128)(2,1)}) %all-gather.11.cloned.1.call-update) | async-done | bytes 1048592 | tf_op jit(solution)/shard_map/all_gather | solution.py:120
  485.4 14.7 collective-permute-done.5
  506.3 9.7 multiply_reduce_fusion.104
  517.6 13.9 collective-permute-done.6
  536.1 12.0 collective-permute-done.7
  548.1 59.9 %all-gather.13.cloned.1.call-done = bf16[128,4096]{1,0:T(8,128)(2,1)} async-done(((bf16[128,2048]{1,0:T(8,128)(2,1)}), bf16[128,4096]{1,0:T(8,128)(2,1)}) %all-gather.13.cloned.1.call-update) | async-done | bytes 1048592 | tf_op jit(solution)/shard_map/all_gather | solution.py:120
  613.9 14.7 collective-permute-done.8
  634.9 9.7 multiply_reduce_fusion.98
  646.2 13.9 collective-permute-done.9
  664.7 12.0 collective-permute-done.10
  676.7 60.7 %all-gather.15.cloned.1.call-done = bf16[128,4096]{1,0:T(8,128)(2,1)} async-done(((bf16[128,2048]{1,0:T(8,128)(2,1)}), bf16[128,4096]{1,0:T(8,128)(2,1)}) %all-gather.15.cloned.1.call-update) | async-done | bytes 1048592 | tf_op jit(solution)/shard_map/all_gather | solution.py:120
  743.5 14.7 collective-permute-done.11
  764.4 9.7 multiply_reduce_fusion.92
  775.8 13.9 collective-permute-done.12
  794.2 12.0 collective-permute-done.13
  806.3 61.5 %all-gather.17.cloned.1.call-done = bf16[128,4096]{1,0:T(8,128)(2,1)} async-done(((bf16[128,2048]{1,0:T(8,128)(2,1)}), bf16[128,4096]{1,0:T(8,128)(2,1)}) %all-gather.17.cloned.1.call-update) | async-done | bytes 1048592 | tf_op jit(solution)/shard_map/all_gather | solution.py:120
  873.6 14.7 collective-permute-done.14
  894.6 9.7 multiply_reduce_fusion.86
  905.9 13.9 collective-permute-done.15
  924.5 12.0 collective-permute-done.16
  936.5 60.6 %all-gather.19.cloned.1.call-done = bf16[128,4096]{1,0:T(8,128)(2,1)} async-done(((bf16[128,2048]{1,0:T(8,128)(2,1)}), bf16[128,4096]{1,0:T(8,128)(2,1)}) %all-gather.19.cloned.1.call-update) | async-done | bytes 1048592 | tf_op jit(solution)/shard_map/all_gather | solution.py:120
  1002.9 14.7 collective-permute-done.17
  1023.9 9.7 multiply_reduce_fusion.80
  1035.2 13.9 collective-permute-done.18
  1053.7 53.6 %collective-permute-done.19 = bf16[128,2048]{1,0:T(8,128)(2,1)} collective-permute-done((bf16[128,2048]{1,0:T(8,128)(2,1)}, bf16[128,2048]{1,0:T(8,128)(2,1)}, u32[]{:S(2)}, u32[]{:S(2)}) %collective-permute-start.19) | collective-permute-done | bytes 524320 | tf_op jit(solution)/shard_map/ppermute | solution.py:10
  1107.4 16.7 %all-gather.21.cloned.1.call-done = bf16[128,4096]{1,0:T(8,128)(2,1)} async-done(((bf16[128,2048]{1,0:T(8,128)(2,1)}), bf16[128,4096]{1,0:T(8,128)(2,1)}) %all-gather.21.cloned.1.call-update) | async-done | bytes 1048592 | tf_op jit(solution)/shard_map/all_gather | solution.py:120
  1124.1 14.4 conditional.42
  1124.4 9.7 fusion.9
  1141.1 14.7 collective-permute-done.20
  1157.2 13.0 conditional.43
  1173.0 9.7 multiply_reduce_fusion.74
  1184.3 13.9 collective-permute-done.21
  1199.3 20.9 %conditional.44 = (bf16[128,2048]{1,0:T(8,128)(2,1)}) conditional(s32[]{:T(128)} %convert_element_type.283, () %tuple.217, (bf16[128,2048]{1,0:T(8,128)(2,1)}, f32[7,3,2048]{2,1,0:T(4,128)S(1)}, f32[3,128,2048]{1,2,0:T(8,128)}, f32[6,2048]{0,1:T(8,128)}) %tuple.258), branch_computations={%region_125.126_spmd, %region_126.134_spmd} | conditional | flops 11796480 | bytes 26026020 | solution.py:175
  1205.7 11.9 multiply_reduce_fusion.47
  1222.1 12.7 collective-permute-done.22
  1265.5 17.8 %copy.355 = f32[128,128,256]{0,2,1:T(8,128)} copy(f32[128,128,256]{2,1,0:T(8,128)} %fusion.30) | data formatting | bytes 33554432 | tf_op jit(solution)/shard_map/reshape | solution.py:29
  1283.3 13.3 pad.28
  1296.6 17.5 %reshape.239 = f32[128,128,257]{0,2,1:T(8,128)} reshape(f32[128,32896]{0,1:T(8,128)} %pad.28) | data formatting | bytes 33685504 | tf_op jit(solution)/shard_map/reshape | solution.py:31
  1324.2 77.1 %psum.15 = bf16[1,128,128]{1,2,0:T(8,128)(2,1)} all-reduce(bf16[1,128,128]{1,2,0:T(8,128)(2,1)} %bitcast.401), channel_id=1, replica_groups=mesh['pipe'=8,'seq'=16,'tp'=2] {'seq'}, use_global_device_ids=true, to_apply=%region_162.163 | all-reduce | flops 16384 | bytes 65536 | tf_op jit(solution)/shard_map/psum | solution.py:212
  1422.5 9.4 multiply_reduce_fusion.68
  1446.5 96.5 %all-reduce.27.cloned.1.call-done = bf16[1,7,3,2048]{3,1,2,0:T(8,128)(2,1)} async-done(((bf16[1,7,3,2048]{3,1,2,0:T(8,128)(2,1)}), bf16[1,7,3,2048]{3,1,2,0:T(8,128)(2,1)}) %all-reduce.27.cloned.1.call-update) | async-done | bytes 86032 | tf_op jit(solution)/shard_map/psum | solution.py:211
  (286 shorter events, 378.0 us)
Async XLA Ops:
  7.2 5.8 copy-start.52
  18.9 11.9 copy-start.65
  18.9 303.2 %all-to-all-start = ((bf16[2048,16,256]{2,0,1:T(8,128)(2,1)}), bf16[2048,16,256]{2,0,1:T(8,128)(2,1)}, u32[]{:S(2)}, u32[]{:S(2)}) async-start(bf16[2048,16,256]{2,0,1:T(8,128)(2,1)} %concatenate.115), calls=%async_computation | async-start | bytes 33554432 | tf_op jit(solution)/shard_map/all_to_all | solution.py:187
  26.1 317.7 %all-gather.9.cloned.1.call-start = ((), (), s32[]{:S(2)}) async-start(), calls=%async_computation.2 | async-start | bytes 1572864 | tf_op jit(solution)/shard_map/all_gather | solution.py:120
  26.9 452.6 %all-gather.11.cloned.1.call-start = ((), (), s32[]{:S(2)}) async-start(), calls=%async_computation.3 | async-start | bytes 1572864 | tf_op jit(solution)/shard_map/all_gather | solution.py:120
  26.9 146.7 %collective-permute-start = (bf16[6,2048]{1,0:T(8,128)(2,1)S(1)}, bf16[6,2048]{1,0:T(8,128)(2,1)S(1)}, u32[]{:S(2)}, u32[]{:S(2)}) collective-permute-start(bf16[6,2048]{1,0:T(8,128)(2,1)S(1)} %slice.757), channel_id=1, source_target_pairs={{0,2},{2,4},{4,6},{6,8},{8,10},{10,12},{12,14},{14,16},{16,18},{18... | collective-permute-start | bytes 73736 | tf_op jit(solution)/shard_map/ppermute | solution.py:10
  55.6 12.6 copy-start.64
  181.7 7.7 copy-start.32
  350.9 16.9 %collective-permute-start.1 = (bf16[127,2048]{0,1:T(8,128)(2,1)}, bf16[127,2048]{0,1:T(8,128)(2,1)}, u32[]{:S(2)}, u32[]{:S(2)}) collective-permute-start(bf16[127,2048]{0,1:T(8,128)(2,1)} %slice.773), channel_id=1, source_target_pairs={{0,2},{2,4},{4,6},{6,8},{8,10},{10,12},{12,14},{14,16},{16,18},{18... | collective-permute-start | bytes 1560584 | tf_op jit(solution)/shard_map/ppermute | solution.py:10
  357.9 14.7 collective-permute-start.2
  373.6 9.6 slice-start
  376.1 7.1 copy-start.1
  376.1 7.1 slice-start.1
  397.8 13.5 collective-permute-start.3
  413.2 13.1 collective-permute-start.4
  426.3 181.7 %all-gather.13.cloned.1.call-start = ((), (), s32[]{:S(2)}) async-start(), calls=%async_computation.4 | async-start | bytes 1572864 | tf_op jit(solution)/shard_map/all_gather | solution.py:120
  484.1 16.0 %collective-permute-start.5 = (bf16[127,2048]{0,1:T(8,128)(2,1)S(1)}, bf16[127,2048]{0,1:T(8,128)(2,1)S(1)}, u32[]{:S(2)}, u32[]{:S(2)}) collective-permute-start(bf16[127,2048]{0,1:T(8,128)(2,1)S(1)} %bitcast.393), channel_id=1, source_target_pairs={{2,0},{4,2},{6,4},{8,6},{10,8},{12,10},{14,12},{16,14},{18,16},{20... | collective-permute-start | bytes 1560584 | tf_op jit(solution)/shard_map/ppermute | solution.py:10
  503.5 2.8 copy-start.8
  516.3 15.2 collective-permute-start.6
  533.4 14.6 collective-permute-start.7
  548.1 189.4 %all-gather.15.cloned.1.call-start = ((), (), s32[]{:S(2)}) async-start(), calls=%async_computation.5 | async-start | bytes 1572864 | tf_op jit(solution)/shard_map/all_gather | solution.py:120
  612.6 16.0 %collective-permute-start.8 = (bf16[127,2048]{0,1:T(8,128)(2,1)S(1)}, bf16[127,2048]{0,1:T(8,128)(2,1)S(1)}, u32[]{:S(2)}, u32[]{:S(2)}) collective-permute-start(bf16[127,2048]{0,1:T(8,128)(2,1)S(1)} %bitcast.394), channel_id=1, source_target_pairs={{2,0},{4,2},{6,4},{8,6},{10,8},{12,10},{14,12},{16,14},{18,16},{20... | collective-permute-start | bytes 1560584 | tf_op jit(solution)/shard_map/ppermute | solution.py:10
  632.0 2.8 copy-start.11
  644.9 15.2 collective-permute-start.9
  662.1 14.6 collective-permute-start.10
  676.7 191.1 %all-gather.17.cloned.1.call-start = ((), (), s32[]{:S(2)}) async-start(), calls=%async_computation.6 | async-start | bytes 1572864 | tf_op jit(solution)/shard_map/all_gather | solution.py:120
  742.2 16.0 %collective-permute-start.11 = (bf16[127,2048]{0,1:T(8,128)(2,1)S(1)}, bf16[127,2048]{0,1:T(8,128)(2,1)S(1)}, u32[]{:S(2)}, u32[]{:S(2)}) collective-permute-start(bf16[127,2048]{0,1:T(8,128)(2,1)S(1)} %bitcast.395), channel_id=1, source_target_pairs={{2,0},{4,2},{6,4},{8,6},{10,8},{12,10},{14,12},{16,14},{18,16},{20... | collective-permute-start | bytes 1560584 | tf_op jit(solution)/shard_map/ppermute | solution.py:10
  774.5 15.2 collective-permute-start.12
  791.6 14.6 collective-permute-start.13
  806.2 190.8 %all-gather.19.cloned.1.call-start = ((), (), s32[]{:S(2)}) async-start(), calls=%async_computation.7 | async-start | bytes 1572864 | tf_op jit(solution)/shard_map/all_gather | solution.py:120
  872.3 16.0 %collective-permute-start.14 = (bf16[127,2048]{0,1:T(8,128)(2,1)S(1)}, bf16[127,2048]{0,1:T(8,128)(2,1)S(1)}, u32[]{:S(2)}, u32[]{:S(2)}) collective-permute-start(bf16[127,2048]{0,1:T(8,128)(2,1)S(1)} %bitcast.396), channel_id=1, source_target_pairs={{2,0},{4,2},{6,4},{8,6},{10,8},{12,10},{14,12},{16,14},{18,16},{20... | collective-permute-start | bytes 1560584 | tf_op jit(solution)/shard_map/ppermute | solution.py:10
  904.6 15.2 collective-permute-start.15
  921.8 14.6 collective-permute-start.16
  936.5 187.6 %all-gather.21.cloned.1.call-start = ((), (), s32[]{:S(2)}) async-start(), calls=%async_computation.8 | async-start | bytes 1572864 | tf_op jit(solution)/shard_map/all_gather | solution.py:120
  1001.6 16.0 %collective-permute-start.17 = (bf16[127,2048]{0,1:T(8,128)(2,1)S(1)}, bf16[127,2048]{0,1:T(8,128)(2,1)S(1)}, u32[]{:S(2)}, u32[]{:S(2)}) collective-permute-start(bf16[127,2048]{0,1:T(8,128)(2,1)S(1)} %bitcast.397), channel_id=1, source_target_pairs={{2,0},{4,2},{6,4},{8,6},{10,8},{12,10},{14,12},{16,14},{18,16},{20... | collective-permute-start | bytes 1560584 | tf_op jit(solution)/shard_map/ppermute | solution.py:10
  1033.9 15.2 collective-permute-start.18
  1051.0 56.3 %collective-permute-start.19 = (bf16[128,2048]{1,0:T(8,128)(2,1)}, bf16[128,2048]{1,0:T(8,128)(2,1)}, u32[]{:S(2)}, u32[]{:S(2)}) collective-permute-start(bf16[128,2048]{1,0:T(8,128)(2,1)} %get-tuple-element.1183), channel_id=1, source_target_pairs={{32,0},{64,32},{96,64},{128,96},{160,128},{192,160},{224,192},{33,... | collective-permute-start | bytes 1572872 | tf_op jit(solution)/shard_map/ppermute | solution.py:10
  1107.3 143.1 %all-gather.23.cloned.1.call-start = ((), (), s32[]{:S(2)}) async-start(), calls=%async_computation.9 | async-start | bytes 1572864 | tf_op jit(solution)/shard_map/all_gather | solution.py:120
  1139.8 16.0 %collective-permute-start.20 = (bf16[127,2048]{0,1:T(8,128)(2,1)S(1)}, bf16[127,2048]{0,1:T(8,128)(2,1)S(1)}, u32[]{:S(2)}, u32[]{:S(2)}) collective-permute-start(bf16[127,2048]{0,1:T(8,128)(2,1)S(1)} %bitcast.398), channel_id=1, source_target_pairs={{2,0},{4,2},{6,4},{8,6},{10,8},{12,10},{14,12},{16,14},{18,16},{20... | collective-permute-start | bytes 1560584 | tf_op jit(solution)/shard_map/ppermute | solution.py:10
  1170.1 2.8 copy-start.23
  1183.0 15.2 collective-permute-start.21
  1205.7 11.9 copy-start.59
  1220.2 14.6 collective-permute-start.22
  1234.8 308.3 %all-reduce.27.cloned.1.call-start = ((), (), s32[]{:S(2)}) async-start(), calls=%async_computation.10 | async-start | bytes 196608 | tf_op jit(solution)/shard_map/psum | solution.py:211
  1253.3 4.0 copy-start.2
  1256.1 149.1 %collective-permute-start.23 = (bf16[127,2048]{0,1:T(8,128)(2,1)}, bf16[127,2048]{0,1:T(8,128)(2,1)}, u32[]{:S(2)}, u32[]{:S(2)}) collective-permute-start(bf16[127,2048]{0,1:T(8,128)(2,1)} %bitcast.352), channel_id=1, source_target_pairs={{2,0},{4,2},{6,4},{8,6},{10,8},{12,10},{14,12},{16,14},{18,16},{20... | collective-permute-start | bytes 1560584 | tf_op jit(solution)/shard_map/ppermute | solution.py:10
  1414.0 5.9 copy-start.50
  1432.3 11.1 collective-permute-start.24
  (18 other events, 37.5 us)
Sparse Core Ops, SparseCore 0:
  28.8 17.0 all-gather.8
  426.4 52.9 all-gather.10
  548.2 59.8 all-gather.12
  676.8 60.5 all-gather.14
  806.3 61.3 all-gather.16
  936.6 60.4 all-gather.18
  1107.4 16.5 all-gather.20
  1234.9 15.4 all-gather.22
  1434.6 108.4 all-reduce.26
